TPU v7x, 32 devices: a whole 2x2x4 slice. The times are simulated.
32 devices in a mesh: row: 8 (over z, core), col: 4 (over y, x).
Axes of the slice: x: 2, y: 2, z: 4, core: 2. Of those that a mesh axis runs over, the one named last changes fastest.
Arguments:
- density: bfloat16 [8192, 8192], P('row', 'col'), may hold values from -6 to 6
- listed: int32 [64, 64], P('row', 'col'), may hold values 0 or 1
- three_centre: bfloat16 [128, 512, 512], P(('row', 'col')), may hold values from -0.25 to 0.25
Outputs:
- exchange_diag: float32 [8192, 512], P('row', 'col')
- exchange_density: bfloat16 [8192, 8192], P('row', 'col')
All inputs are finite; a program needn't handle non-finite values. No bound on the sum of `listed` on one device may be relied on, other than what follows from the above.
Results may differ from a plain program's by a relative error of at most 0.0058.
Values may be sent and summed in bfloat16 or wider, within the bound.
A program may use at most 64 MiB of HBM per device.

v0:
```python
import jax
import jax.numpy as jnp
from jax import lax
from jax.sharding import PartitionSpec as P

TILE = 128
W = 512


def from_root(value, axis, root):
    mine = lax.axis_index(axis) == root
    return lax.psum(jnp.where(mine, value, jnp.zeros_like(value)), axis)


def partner_2(block, axis, stride):
    count = lax.axis_size(axis)
    route = []
    for low in range(count):
        high = low | 1 << stride
        if high != low and high < count:
            route += [(low, high), (high, low)]
    return lax.ppermute(block, axis, route)


def halve_rows(values, row_index, levels, sender):
    for bit_level in reversed(range(levels)):
        middle = values.shape[0] // 2
        lower_half = row_index // 2**bit_level % 2 == 0
        kept_rows = jnp.where(lower_half, values[:middle], values[middle:])
        sent_rows = jnp.where(lower_half, values[middle:], values[:middle])
        values = kept_rows + sender(sent_rows, bit_level)
    return values


def per_device(density, listed, three_centre):
    tile_rows = listed.shape[0]
    tile_cols = listed.shape[1]
    quad_tiles = max(tile_rows, 4)
    groups_dev = quad_tiles // 4
    aux_count = three_centre.shape[0]
    col_count = lax.axis_size("col")
    row_index = lax.axis_index("row")
    col_index = lax.axis_index("col")
    masked = (
        density.reshape(tile_rows, TILE, tile_cols, TILE)
        * listed[:, None, :, None].astype(jnp.bfloat16)
    ).reshape(tile_rows * TILE, tile_cols * TILE)
    quad_start = row_index * tile_rows // quad_tiles * quad_tiles
    col_offset = quad_start % tile_cols * TILE
    portion = lax.dynamic_slice_in_dim(masked, col_offset, quad_tiles * TILE, 1)
    diagonal = from_root(portion, "col", quad_start // tile_cols)
    joined = jnp.concatenate([diagonal, masked], axis=1)
    levels = (quad_tiles // tile_rows).bit_length() - 1
    for bit_level in range(levels):
        partner = partner_2(joined, "row", bit_level)
        lower_half = row_index // 2**bit_level % 2 == 0
        joined = jnp.where(
            lower_half,
            jnp.concatenate([joined, partner], axis=0),
            jnp.concatenate([partner, joined], axis=0),
        )
    quad_block = joined[:, : quad_tiles * TILE]
    quad_density = joined[:, quad_tiles * TILE :]
    group_ids = jnp.arange(groups_dev, dtype=jnp.int32)
    exchange_quad = jnp.zeros((groups_dev, W, W), jnp.float32)
    for aux_slot in range(aux_count):
        group_slot = (col_index * aux_count + aux_slot) % groups_dev
        density_sub = lax.dynamic_slice(quad_block, (group_slot * W, group_slot * W), (W, W))
        aux_block = three_centre[aux_slot]
        half_product = jnp.dot(aux_block, density_sub, preferred_element_type=jnp.float32).astype(
            jnp.bfloat16
        )
        contribution = lax.dot_general(
            half_product, aux_block, (((1,), (1,)), ((), ())), preferred_element_type=jnp.float32
        )
        exchange_quad = exchange_quad + jnp.where(
            (group_ids == group_slot)[:, None, None], contribution[None], 0.0
        )
    aux_group = aux_count * col_count * 4 // tile_rows
    exchange_quad = (exchange_quad * aux_group ** (-0.5)).reshape(quad_tiles * TILE, W)
    column_share = lax.psum_scatter(exchange_quad, "col", scatter_dimension=1, tiled=True)
    exchange_diag = halve_rows(
        column_share,
        row_index,
        levels,
        lambda sent_rows, bit_level: partner_2(sent_rows, "row", bit_level),
    )
    fock_rounded = lax.all_gather(exchange_diag.astype(jnp.bfloat16), "col", axis=1, tiled=True)
    rows_here = tile_rows * TILE
    segment_rows = min(rows_here, W)
    segment_count = rows_here // segment_rows
    within_quad = (row_index * tile_rows - quad_start) * TILE
    products = []
    for segment in range(segment_count):
        group_position = (within_quad + segment * segment_rows) // W
        dens_rows = lax.dynamic_slice_in_dim(quad_density, group_position * W, W, 0)
        fock_part = fock_rounded[segment * segment_rows : (segment + 1) * segment_rows]
        products.append(
            jnp.dot(fock_part, dens_rows, preferred_element_type=jnp.float32) * W ** (-0.5)
        )
    exchange_density = jnp.concatenate(products, axis=0).astype(jnp.bfloat16)
    return (exchange_diag, exchange_density)


def solution(mesh):
    placed = (P("row", "col"), P("row", "col"), P(("row", "col"), None, None))
    return jax.shard_map(
        per_device,
        mesh=mesh,
        in_specs=placed,
        out_specs=(P("row", "col"), P("row", "col")),
        check_vma=False,
    )
```

profile of v0, /device:TPU:0, one launch (start us, length us, event | category | flops | bytes accessed | tf_op | source)
XLA Modules:
  0.0 177.6 jit_solution(2169298815006904635)
XLA Ops:
  7.2 0.0 all-reduce.2.cloned.1.call-start
  7.3 0.7 convert_element_type.24
  7.9 0.0 copy-start.2
  8.0 0.6 mul.68
  8.6 1.6 copy-done.2
  10.1 0.9 bitcast_multiply_fusion
  11.0 0.0 copy-start
  11.1 2.0 %copy-done = bf16[1024,2048]{1,0:T(8,128)(2,1)} copy-done((bf16[1024,2048]{1,0:T(8,128)(2,1)}, bf16[1024,2048]{1,0:T(8,128)(2,1)S(1)}, u32[]{:S(2)}) %copy-start) | copy-done | bytes 4194328
  13.1 1.9 %dynamic-slice_select_fusion = bf16[1024,1024]{1,0:T(8,128)(2,1)} fusion(bf16[1024,2048]{1,0:T(8,128)(2,1)S(1)} %bitcast_multiply_fusion, s32[]{:T(128)S(6)} %select_n.91, pred[]{:T(512)S(6)} %eq.51), kind=kLoop, calls=%fused_computation.14 | loop fusion | flops 1048576 | bytes 4194309 | tf_op jit(solution)/shard_map/jit(_where)/select_n | solution.py:12
  14.9 0.0 copy-start.3
  14.9 0.0 all-reduce.2.cloned.1.call-update
  14.9 0.0 reduce-scatter.2.cloned.1.call-start
  15.1 0.1 broadcast_in_dim.101
  15.2 0.1 broadcast_in_dim.106
  15.3 0.1 broadcast_in_dim.96
  15.4 0.1 broadcast_in_dim.89
  15.5 71.9 %all-reduce.2.cloned.1.call-done = bf16[1024,1024]{1,0:T(8,128)(2,1)} async-done(((bf16[1024,1024]{1,0:T(8,128)(2,1)}), bf16[1024,1024]{1,0:T(8,128)(2,1)}) %all-reduce.2.cloned.1.call-update) | async-done | bytes 2097168 | tf_op jit(solution)/shard_map/psum | solution.py:12
  87.3 0.0 copy-done.3
  87.3 1.9 %fusion.7 = f32[512,512]{1,0:T(8,128)S(1)} fusion(bf16[4,512,512]{2,1,0:T(8,128)(2,1)S(1)} %copy-done.3, bf16[1024,1024]{1,0:T(8,128)(2,1)} %all-reduce.2.cloned.1.call-done, s32[]{:T(128)S(6)} %select_n.96), kind=kOutput, calls=%fused_computation.20 | convolution fusion | flops 537133056 | bytes 2621444 | tf_op jit(solution)/shard_map/dot_general | solution.py:73
  89.2 2.2 %fusion.8 = f32[512,512]{1,0:T(8,128)S(1)} fusion(bf16[4,512,512]{2,1,0:T(8,128)(2,1)} %param.5, bf16[1024,1024]{1,0:T(8,128)(2,1)} %all-reduce.2.cloned.1.call-done, s32[]{:T(128)S(6)} %select_n.99), kind=kOutput, calls=%fused_computation.21 | convolution fusion | flops 537133056 | bytes 2621444 | tf_op jit(solution)/shard_map/dot_general | solution.py:73
  91.5 2.2 %fusion.6 = f32[512,512]{1,0:T(8,128)S(1)} fusion(bf16[4,512,512]{2,1,0:T(8,128)(2,1)} %param.5, bf16[1024,1024]{1,0:T(8,128)(2,1)} %all-reduce.2.cloned.1.call-done, s32[]{:T(128)S(6)} %select_n.93), kind=kOutput, calls=%fused_computation.19 | convolution fusion | flops 537133056 | bytes 2621444 | tf_op jit(solution)/shard_map/dot_general | solution.py:73
  93.7 3.2 %fusion.9 = f32[512,512]{1,0:T(8,128)} fusion(bf16[4,512,512]{2,1,0:T(8,128)(2,1)} %param.5, bf16[1024,1024]{1,0:T(8,128)(2,1)} %all-reduce.2.cloned.1.call-done, s32[]{:T(128)S(6)} %select_n.102), kind=kOutput, calls=%fused_computation.22 | convolution fusion | flops 537133056 | bytes 2621444 | tf_op jit(solution)/shard_map/dot_general | solution.py:73
  96.9 3.3 %fusion.1 = f32[1024,512]{1,0:T(8,128)} fusion(f32[512,512]{1,0:T(8,128)} %fusion.9, f32[512,512]{1,0:T(8,128)S(1)} %fusion.8, f32[512,512]{1,0:T(8,128)S(1)} %fusion.7, f32[512,512]{1,0:T(8,128)S(1)} %fusion.6, pred[1024]{0:T(1024)(128)(4,1)S(1)} %broadcast_in_dim.107, pred[1024]{0:T(1024)(128)(4,1)S(1)} %broadcast_in_dim.102, ...), kind=kLoop, calls=%fused_computation.6 | loop fusion | flops 4194304 | bytes 6295552 | tf_op jit(solution)/shard_map/mul | solution.py:80
  100.2 0.0 reduce-scatter.2.cloned.1.call-update
  100.2 0.0 all-gather.2.cloned.1.call-start
  100.3 35.3 %reduce-scatter.2.cloned.1.call-done = f32[1024,128]{1,0:T(8,128)} async-done(((f32[1024,512]{1,0:T(8,128)}), f32[1024,128]{1,0:T(8,128)}) %reduce-scatter.2.cloned.1.call-update) | async-done | bytes 524304 | tf_op jit(solution)/shard_map/reduce_scatter | solution.py:81
  135.6 1.8 %convert_element_type.29 = bf16[1024,128]{1,0:T(8,128)(2,1)} convert(f32[1024,128]{1,0:T(8,128)} %reduce-scatter.2.cloned.1.call-done) | non-fusion elementwise | flops 131072 | bytes 786432 | tf_op jit(solution)/shard_map/convert_element_type | solution.py:88
  137.3 0.0 all-gather.2.cloned.1.call-update
  137.4 26.5 %all-gather.2.cloned.1.call-done = bf16[1024,512]{1,0:T(8,128)(2,1)} async-done(((bf16[1024,128]{1,0:T(8,128)(2,1)}), bf16[1024,512]{1,0:T(8,128)(2,1)}) %all-gather.2.cloned.1.call-update) | async-done | bytes 1048592 | tf_op jit(solution)/shard_map/all_gather | solution.py:88
  163.9 0.0 copy-start.1
  163.9 0.0 copy-start.4
  163.9 3.2 %multiply_convert_fusion.1 = bf16[512,2048]{1,0:T(8,128)(2,1)S(1)} fusion(bf16[1024,2048]{1,0:T(8,128)(2,1)} %copy-done, s32[]{:T(128)S(6)} %select_n.105, bf16[1024,512]{1,0:T(8,128)(2,1)} %all-gather.2.cloned.1.call-done), kind=kOutput, calls=%fused_computation.3 | convolution fusion | flops 1075838976 | bytes 4718596 | tf_op jit(solution)/shard_map/dot_general | solution.py:99
  167.1 0.0 copy-done.1
  167.1 0.1 copy-done.4
  167.2 1.3 multiply_convert_fusion
  168.4 2.6 %pad_maximum_fusion = bf16[1024,2048]{1,0:T(8,128)(2,1)} fusion(bf16[512,2048]{1,0:T(8,128)(2,1)S(1)} %multiply_convert_fusion, bf16[512,2048]{1,0:T(8,128)(2,1)S(1)} %multiply_convert_fusion.1), kind=kLoop, calls=%fused_computation.1 | loop fusion | flops 8388608 | bytes 8388608 | tf_op jit(solution)/shard_map/concatenate | solution.py:101
  (8 shorter events, 0.1 us)
Async XLA Ops:
  7.2 80.1 %all-reduce.2.cloned.1.call-start = ((), (), s32[]{:S(2)}) async-start(), calls=%async_computation.1 | async-start | bytes 4194304 | tf_op jit(solution)/shard_map/psum | solution.py:12
  7.9 2.2 %copy-start.2 = (bf16[1024,2048]{1,0:T(8,128)(2,1)S(1)}, bf16[1024,2048]{1,0:T(8,128)(2,1)}, u32[]{:S(2)}) copy-start(bf16[1024,2048]{1,0:T(8,128)(2,1)} %param.3) | copy-start | bytes 12582916
  11.0 2.0 %copy-start = (bf16[1024,2048]{1,0:T(8,128)(2,1)}, bf16[1024,2048]{1,0:T(8,128)(2,1)S(1)}, u32[]{:S(2)}) copy-start(bf16[1024,2048]{1,0:T(8,128)(2,1)S(1)} %bitcast_multiply_fusion) | copy-start | bytes 12582916
  14.9 72.4 %copy-start.3 = (bf16[4,512,512]{2,1,0:T(8,128)(2,1)S(1)}, bf16[4,512,512]{2,1,0:T(8,128)(2,1)}, u32[]{:S(2)}) copy-start(bf16[4,512,512]{2,1,0:T(8,128)(2,1)} %param.5) | copy-start | bytes 6291460
  14.9 120.6 %reduce-scatter.2.cloned.1.call-start = ((), (), s32[]{:S(2)}) async-start(), calls=%async_computation.2 | async-start | bytes 2621440 | tf_op jit(solution)/shard_map/reduce_scatter | solution.py:81
  100.2 63.7 %all-gather.2.cloned.1.call-start = ((), (), s32[]{:S(2)}) async-start(), calls=%async_computation.3 | async-start | bytes 1310720 | tf_op jit(solution)/shard_map/all_gather | solution.py:88
  163.9 3.2 %copy-start.1 = (bf16[1024,2048]{1,0:T(8,128)(2,1)S(1)}, bf16[1024,2048]{1,0:T(8,128)(2,1)}, u32[]{:S(2)}) copy-start(bf16[1024,2048]{1,0:T(8,128)(2,1)} %copy-done) | copy-start | bytes 12582916
  163.9 3.3 %copy-start.4 = (bf16[1024,512]{1,0:T(8,128)(2,1)S(1)}, bf16[1024,512]{1,0:T(8,128)(2,1)}, u32[]{:S(2)}) copy-start(bf16[1024,512]{1,0:T(8,128)(2,1)} %all-gather.2.cloned.1.call-done) | copy-start | bytes 3145732
Sparse Core Ops, SparseCore 0:
  15.1 72.1 all-reduce.1
  100.3 35.1 reduce-scatter.1
  137.5 26.3 all-gather.1
where the time goes:
time: 178 us
  waiting for transfers between devices  134 us (75%)
  matrix products  14 us (8%)
  between operations  14 us (8%)
  other arithmetic  11.1 us (6%)
  local copies, waits for them, and re-layouts  4.68 us (3%)
    psum x1, waiting for transfers between devices, from_root(): return lax.psum(jnp.where(mine, value, jnp.zeros_like(value)), axis)  71.9 us
    reduce_scatter x1, waiting for transfers between devices, per_device(): lax.psum_scatter(exchange_quad, 'col', scatter_dimension=1, tiled=True)  35.3 us
    all_gather x1, waiting for transfers between devices, per_device(): lax.all_gather(exchange_diag.astype(jnp.bfloat16), 'col', axis=1, tiled=T...  26.5 us
    dot_general x4, matrix products, per_device(): lax.dot_general(half_product, aux_block, (((1,), (1,)), ((), ())), prefer...  9.58 us
    dot_general x2, matrix products, per_device(): jnp.dot(fock_part, dens_rows, preferred_element_type=jnp.float32)  4.42 us
    unnamed x10, local copies, waits for them, and re-layouts  3.68 us
  transfers between devices with their start and end apart: 3, of which 3 were waited for; matrix products, arithmetic and copies ran while one was open for 0% of the time, Pallas kernels for 0%

commit v1 on v0

--- a/solution.py
+++ b/solution.py
@@ -9,7 +9,7 @@
 
 def from_root(value, axis, root):
     mine = lax.axis_index(axis) == root
-    return lax.psum(jnp.where(mine, value, jnp.zeros_like(value)), axis)
+    return jnp.sum(lax.all_gather(jnp.where(mine, value, jnp.zeros_like(value)), axis), axis=0)
 
 
 def partner_2(block, axis, stride):

time: 178 us -> 205 us (1.15)
  waiting for transfers between devices: 134 us -> 152 us
  other arithmetic: 11.1 us -> 18.3 us
    all_gather x0 -> x1, waiting for transfers between devices: none -> 89.8 us  [from_root(): lax.all_gather(jnp.where(mine, value, jnp.zeros_like(value)), axis)]
    psum x1 -> x0, waiting for transfers between devices: 71.9 us -> none  [from_root(): return lax.psum(jnp.where(mine, value, jnp.zeros_like(value)), axis)]
    reduce_sum x0 -> x1, other arithmetic: none -> 6.5 us  [from_root(): jnp.sum(lax.all_gather(jnp.where(mine, value, jnp.zeros_like(value)), axi...]
where the time goes in v1:
time: 205 us; the launch traced here: 204 us
  waiting for transfers between devices  152 us (74%)
  other arithmetic  18.3 us (9%)
  matrix products  15.6 us (8%)
  between operations  13.9 us (7%)
  local copies, waits for them, and re-layouts  4.67 us (2%)
    all_gather x1, waiting for transfers between devices, from_root(): lax.all_gather(jnp.where(mine, value, jnp.zeros_like(value)), axis)  89.8 us
    reduce_scatter x1, waiting for transfers between devices, per_device(): lax.psum_scatter(exchange_quad, 'col', scatter_dimension=1, tiled=True)  35.3 us
    all_gather x1, waiting for transfers between devices, per_device(): lax.all_gather(exchange_diag.astype(jnp.bfloat16), 'col', axis=1, tiled=T...  26.5 us
    dot_general x4, matrix products, per_device(): lax.dot_general(half_product, aux_block, (((1,), (1,)), ((), ())), prefer...  11.2 us
    reduce_sum x1, other arithmetic, from_root(): jnp.sum(lax.all_gather(jnp.where(mine, value, jnp.zeros_like(value)), axi...  6.5 us
    dot_general x2, matrix products, per_device(): jnp.dot(fock_part, dens_rows, preferred_element_type=jnp.float32)  4.42 us
  transfers between devices with their start and end apart: 3, of which 3 were waited for; matrix products, arithmetic and copies ran while one was open for 0% of the time, Pallas kernels for 0%

profile of v1, /device:TPU:0, one launch (start us, length us, event | category | flops | bytes accessed | tf_op | source)
XLA Modules:
  0.0 204.4 jit_solution(17312574469488372210)
XLA Ops:
  7.2 0.0 all-gather.6.cloned.1.call-start
  7.3 0.7 convert_element_type.26
  7.9 0.0 copy-start.2
  8.0 0.6 mul.68
  8.6 1.6 copy-done.2
  10.1 0.9 bitcast_multiply_fusion
  11.0 0.0 copy-start
  11.1 2.0 copy-done
  13.1 1.9 dynamic-slice_select_fusion
  15.0 0.0 all-gather.6.cloned.1.call-update
  15.0 0.0 reduce-scatter.2.cloned.1.call-start
  15.1 0.1 broadcast_in_dim.101
  15.2 0.1 broadcast_in_dim.106
  15.3 0.1 broadcast_in_dim.96
  15.4 0.1 broadcast_in_dim.89
  15.5 89.8 %all-gather.6.cloned.1.call-done = bf16[4096,1024]{1,0:T(8,128)(2,1)} async-done(((bf16[1024,1024]{1,0:T(8,128)(2,1)}), bf16[4096,1024]{1,0:T(8,128)(2,1)}) %all-gather.6.cloned.1.call-update) | async-done | bytes 8388624 | tf_op jit(solution)/shard_map/all_gather | solution.py:12
  105.4 6.5 %reduce_sum.12 = bf16[1024,1024]{1,0:T(8,128)(2,1)S(1)} reduce(bf16[4,1024,1024]{2,1,0:T(8,128)(2,1)} %bitcast.44, bf16[]{:T(256)} %constant.98.clone.1), dimensions={0}, to_apply=%region_0.1 | reduce | flops 3145728 | bytes 10485762 | tf_op jit(solution)/shard_map/reduce_sum | solution.py:12
  111.9 2.1 %fusion.7 = f32[512,512]{1,0:T(8,128)S(1)} fusion(bf16[4,512,512]{2,1,0:T(8,128)(2,1)} %param.5, bf16[1024,1024]{1,0:T(8,128)(2,1)S(1)} %reduce_sum.12, s32[]{:T(128)S(6)} %select_n.96), kind=kOutput, calls=%fused_computation.20 | convolution fusion | flops 537133056 | bytes 2621444 | tf_op jit(solution)/shard_map/dot_general | solution.py:73
  113.9 3.1 %fusion.8 = f32[512,512]{1,0:T(8,128)} fusion(bf16[4,512,512]{2,1,0:T(8,128)(2,1)} %param.5, bf16[1024,1024]{1,0:T(8,128)(2,1)S(1)} %reduce_sum.12, s32[]{:T(128)S(6)} %select_n.99), kind=kOutput, calls=%fused_computation.21 | convolution fusion | flops 537133056 | bytes 2621444 | tf_op jit(solution)/shard_map/dot_general | solution.py:73
  117.0 3.0 %fusion.6 = f32[512,512]{1,0:T(8,128)} fusion(bf16[4,512,512]{2,1,0:T(8,128)(2,1)} %param.5, bf16[1024,1024]{1,0:T(8,128)(2,1)S(1)} %reduce_sum.12, s32[]{:T(128)S(6)} %select_n.93), kind=kOutput, calls=%fused_computation.19 | convolution fusion | flops 537133056 | bytes 2621444 | tf_op jit(solution)/shard_map/dot_general | solution.py:73
  120.0 3.1 %fusion.9 = f32[512,512]{1,0:T(8,128)} fusion(bf16[4,512,512]{2,1,0:T(8,128)(2,1)} %param.5, bf16[1024,1024]{1,0:T(8,128)(2,1)S(1)} %reduce_sum.12, s32[]{:T(128)S(6)} %select_n.102), kind=kOutput, calls=%fused_computation.22 | convolution fusion | flops 537133056 | bytes 2621444 | tf_op jit(solution)/shard_map/dot_general | solution.py:73
  123.1 3.9 %fusion.1 = f32[1024,512]{1,0:T(8,128)} fusion(f32[512,512]{1,0:T(8,128)} %fusion.9, f32[512,512]{1,0:T(8,128)} %fusion.8, f32[512,512]{1,0:T(8,128)S(1)} %fusion.7, f32[512,512]{1,0:T(8,128)} %fusion.6, pred[1024]{0:T(1024)(128)(4,1)S(1)} %broadcast_in_dim.107, pred[1024]{0:T(1024)(128)(4,1)S(1)} %broadcast_in_dim.102, ...), kind=kLoop, calls=%fused_computation.6 | loop fusion | flops 4194304 | bytes 6295552 | tf_op jit(solution)/shard_map/mul | solution.py:80
  127.0 0.0 reduce-scatter.2.cloned.1.call-update
  127.0 0.0 all-gather.4.cloned.1.call-start
  127.1 35.3 %reduce-scatter.2.cloned.1.call-done = f32[1024,128]{1,0:T(8,128)} async-done(((f32[1024,512]{1,0:T(8,128)}), f32[1024,128]{1,0:T(8,128)}) %reduce-scatter.2.cloned.1.call-update) | async-done | bytes 524304 | tf_op jit(solution)/shard_map/reduce_scatter | solution.py:81
  162.4 1.8 convert_element_type.31
  164.1 0.0 all-gather.4.cloned.1.call-update
  164.2 26.5 %all-gather.4.cloned.1.call-done = bf16[1024,512]{1,0:T(8,128)(2,1)} async-done(((bf16[1024,128]{1,0:T(8,128)(2,1)}), bf16[1024,512]{1,0:T(8,128)(2,1)}) %all-gather.4.cloned.1.call-update) | async-done | bytes 1048592 | tf_op jit(solution)/shard_map/all_gather | solution.py:88
  190.7 0.0 copy-start.1
  190.7 0.0 copy-start.3
  190.7 3.2 %multiply_convert_fusion.1 = bf16[512,2048]{1,0:T(8,128)(2,1)S(1)} fusion(bf16[1024,2048]{1,0:T(8,128)(2,1)} %copy-done, s32[]{:T(128)S(6)} %select_n.105, bf16[1024,512]{1,0:T(8,128)(2,1)} %all-gather.4.cloned.1.call-done), kind=kOutput, calls=%fused_computation.3 | convolution fusion | flops 1075838976 | bytes 4718596 | tf_op jit(solution)/shard_map/dot_general | solution.py:99
  193.8 0.0 copy-done.1
  193.9 0.1 copy-done.3
  194.0 1.3 multiply_convert_fusion
  195.2 2.6 %pad_maximum_fusion = bf16[1024,2048]{1,0:T(8,128)(2,1)} fusion(bf16[512,2048]{1,0:T(8,128)(2,1)S(1)} %multiply_convert_fusion, bf16[512,2048]{1,0:T(8,128)(2,1)S(1)} %multiply_convert_fusion.1), kind=kLoop, calls=%fused_computation.1 | loop fusion | flops 8388608 | bytes 8388608 | tf_op jit(solution)/shard_map/concatenate | solution.py:101
  (8 shorter events, 0.1 us)
Async XLA Ops:
  7.2 98.2 %all-gather.6.cloned.1.call-start = ((), (), s32[]{:S(2)}) async-start(), calls=%async_computation.3 | async-start | bytes 10485760 | tf_op jit(solution)/shard_map/all_gather | solution.py:12
  7.9 2.2 %copy-start.2 = (bf16[1024,2048]{1,0:T(8,128)(2,1)S(1)}, bf16[1024,2048]{1,0:T(8,128)(2,1)}, u32[]{:S(2)}) copy-start(bf16[1024,2048]{1,0:T(8,128)(2,1)} %param.3) | copy-start | bytes 12582916
  11.0 2.0 copy-start
  15.0 147.4 %reduce-scatter.2.cloned.1.call-start = ((), (), s32[]{:S(2)}) async-start(), calls=%async_computation.1 | async-start | bytes 2621440 | tf_op jit(solution)/shard_map/reduce_scatter | solution.py:81
  127.0 63.6 %all-gather.4.cloned.1.call-start = ((), (), s32[]{:S(2)}) async-start(), calls=%async_computation.2 | async-start | bytes 1310720 | tf_op jit(solution)/shard_map/all_gather | solution.py:88
  190.7 3.2 %copy-start.1 = (bf16[1024,2048]{1,0:T(8,128)(2,1)S(1)}, bf16[1024,2048]{1,0:T(8,128)(2,1)}, u32[]{:S(2)}) copy-start(bf16[1024,2048]{1,0:T(8,128)(2,1)} %copy-done) | copy-start | bytes 12582916
  190.7 3.3 %copy-start.3 = (bf16[1024,512]{1,0:T(8,128)(2,1)S(1)}, bf16[1024,512]{1,0:T(8,128)(2,1)}, u32[]{:S(2)}) copy-start(bf16[1024,512]{1,0:T(8,128)(2,1)} %all-gather.4.cloned.1.call-done) | copy-start | bytes 3145732
Sparse Core Ops, SparseCore 0:
  15.1 90.1 all-gather.5
  127.2 35.1 reduce-scatter.1
  164.3 26.3 all-gather.3
